TPU v7x, 32 devices: a whole 2x2x4 slice. The times are simulated.
32 devices in a mesh: curve: 8 (over y, x, core), sub: 4 (over z).
Axes of the slice: x: 2, y: 2, z: 4, core: 2. Of those that a mesh axis runs over, the one named last changes fastest.
Arguments:
- populations: float32 [19, 2048, 256], P(None, ('curve', 'sub')), may hold values from 0.2 to 1.8
- count_old: int32 [8, 4], replicated, may hold values from 2 to 4, as said below
- count_new: int32 [8, 4], replicated, may hold values from 2 to 4, as said below
Outputs:
- evolved: float32 [19, 2048, 256], P(None, ('curve', 'sub'))
Inputs may be any that keep to these rules, and one draw needn't show every extreme that they name: Each row of count_old sums to 3 times the number of devices along sub, so the blocks of a curve segment stay within it; every row has an entry 4. Each row of count_new sums to 3 times the number of devices along sub and has an entry 4. Between count_old and count_new each boundary between the runs of two neighbouring devices moves by at most one block, and in every row one boundary moves, so every block's new owner is its old owner or the device beside it on sub.
All inputs are finite; a program needn't handle non-finite values.
Results may differ from a plain program's by a relative error of at most 0.00002.
Values sent between devices are 32-bit elements; how exact they have to be, the bound alone decides.
No kernel may reach another device: no remote copies, remote signals or barrier semaphores. Data moves between devices by JAX's collectives and lax.ppermute only.
A program may use at most 64 MiB of HBM per device.

v0:
```python
import functools

import jax
import jax.numpy as jnp
import numpy as np
from jax import lax
from jax.experimental import pallas as pl
from jax.experimental.pallas import tpu as pltpu
from jax.sharding import PartitionSpec as P

BX = 16
BZ = 16
STEPS = 4
DIRS = 19
REACH = BX + STEPS
LANES = 128
HALVES = 2
PAD = 8
STRIP = 40
LEFT_EDGE = 32

VELOCITY = np.array(
    [
        [0, 0, 0],
        [1, 0, 0],
        [1, 1, 0],
        [1, -1, 0],
        [1, 0, 1],
        [1, 0, -1],
        [-1, 0, 0],
        [-1, 1, 0],
        [-1, -1, 0],
        [-1, 0, 1],
        [-1, 0, -1],
        [0, 1, 0],
        [0, -1, 0],
        [0, 0, 1],
        [0, 0, -1],
        [0, 1, 1],
        [0, 1, -1],
        [0, -1, 1],
        [0, -1, -1],
    ]
)
tau_base = 0.6
smagorinsky = 0.17


def collide(h):
    def pair(first, second):
        return h[first] + h[second], h[first] - h[second]

    s_x, d_x = pair(1, 6)
    s_xyp, d_xyp = pair(2, 8)
    s_xym, d_xym = pair(3, 7)
    s_xzp, d_xzp = pair(4, 10)
    s_xzm, d_xzm = pair(5, 9)
    s_y, d_y = pair(11, 12)
    s_z, d_z = pair(13, 14)
    s_yzp, d_yzp = pair(15, 18)
    s_yzm, d_yzm = pair(16, 17)
    j_x = (d_x + d_x) + (d_xyp + d_xym) + (d_xzp + d_xzm)
    j_y = (d_y + d_y) + (d_xyp - d_xym) + (d_yzp + d_yzm)
    j_z = (d_z + d_z) + (d_xzp - d_xzm) + (d_yzp - d_yzm)
    t_xy, t_xz, t_yz = s_xyp + s_xym, s_xzp + s_xzm, s_yzp + s_yzm
    m_xy, m_xz, m_yz = s_xyp - s_xym, s_xzp - s_xzm, s_yzp - s_yzm
    ss_x, ss_y, ss_z = s_x + s_x, s_y + s_y, s_z + s_z
    yz_part = ss_y + t_yz
    m_xx = ss_x + (t_xy + t_xz)
    m_yy = yz_part + t_xy
    m_zz = ss_z + (t_xz + t_yz)
    rho36 = (12.0 * h[0] + ss_z) + (m_xx + yz_part)
    inverse = 1.0 / rho36
    k_u = 1.5 * inverse
    k_p = 2.25 * inverse
    u_x, u_y, u_z = j_x * k_u, j_y * k_u, j_z * k_u
    xx, yy, zz = u_x * u_x, u_y * u_y, u_z * u_z
    xy, xz, yz = u_x * u_y, u_x * u_z, u_y * u_z
    p_xx = m_xx * k_p - (xx + 0.75)
    p_yy = m_yy * k_p - (yy + 0.75)
    p_zz = m_zz * k_p - (zz + 0.75)
    p_xy = m_xy * k_p - xy
    p_xz = m_xz * k_p - xz
    p_yz = m_yz * k_p - yz
    off = p_xy * p_xy + p_xz * p_xz + p_yz * p_yz
    square = (p_xx * p_xx + p_yy * p_yy) + (p_zz * p_zz + (off + off))
    magnitude = jnp.sqrt(square)
    factor = 18.0 * np.sqrt(2.0) * smagorinsky * smagorinsky / 2.25
    inner = tau_base * tau_base + float(factor) * magnitude
    omega = 2.0 / (tau_base + inner * lax.rsqrt(inner))
    keep = 1.0 - omega
    gain = (omega * (1.0 / 36.0)) * rho36
    gain2 = gain + gain
    rest = gain - gain * ((2.0 / 3.0) * ((xx + yy) + zz))
    gain4 = gain2 + gain2
    a_x, a_y, a_z = gain2 * u_x, gain2 * u_y, gain2 * u_z
    b_x, b_y, b_z = a_x * u_x, a_y * u_y, a_z * u_z
    n_x, n_y, n_z = rest + b_x, rest + b_y, rest + b_z
    out = [None] * DIRS
    out[0] = keep * h[0] + rest

    def spread(first, second, even, odd):
        out[first] = keep * h[first] + (even + odd)
        out[second] = keep * h[second] + (even - odd)

    spread(1, 6, n_x, a_x)
    spread(11, 12, n_y, a_y)
    spread(13, 14, n_z, a_z)
    for plus, minus, base, cross, first, second in (
        ((2, 8), (3, 7), n_x + b_y, gain4 * xy, a_x, a_y),
        ((4, 10), (5, 9), n_x + b_z, gain4 * xz, a_x, a_z),
        ((15, 18), (16, 17), n_y + b_z, gain4 * yz, a_y, a_z),
    ):
        spread(*plus, base + cross, first + second)
        spread(*minus, base - cross, first - second)
    return out


def lane_sources(step_y, step_z):
    lane = lax.broadcasted_iota(jnp.int32, (8, LANES), 1)
    along_y = (lane - step_y * BZ) & (LANES - 1) & ~(BZ - 1)
    along_z = (lane - step_z) & (BZ - 1)
    return along_y | along_z


def moves():
    lane = lax.broadcasted_iota(jnp.int32, (8, LANES), 1)
    index = {}
    for step_y in (-1, 0, 1):
        for step_z in (-1, 1):
            index[step_y, step_z] = lane_sources(step_y, step_z)
    border = {1: lane < BZ, -1: lane >= LANES - BZ}
    return index, border


def shift_cross(lower, upper, direction, tables):
    index, border = tables
    step_y, step_z = int(VELOCITY[direction, 1]), int(VELOCITY[direction, 2])
    if step_z != 0:
        source = index[step_y, step_z]
        lower = jnp.take_along_axis(lower, source, axis=1, mode="promise_in_bounds")
        upper = jnp.take_along_axis(upper, source, axis=1, mode="promise_in_bounds")
    elif step_y != 0:
        lower = pltpu.roll(lower, (step_y * BZ) % LANES, 1)
        upper = pltpu.roll(upper, (step_y * BZ) % LANES, 1)
    if step_y != 0:
        edge = border[step_y]
        lower, upper = jnp.where(edge, upper, lower), jnp.where(edge, lower, upper)
    return lower, upper


def layout_of(sub_count, old_ref, new_ref, curve, sub):
    old_start, new_start = 0, 0
    for other in range(sub_count - 1):
        before = other < sub
        old_start += jnp.where(before, old_ref[other, curve], 0)
        new_start += jnp.where(before, new_ref[other, curve], 0)
    held_old = old_ref[sub, curve] * BX
    held_new = new_ref[sub, curve] * BX
    return held_old, held_new, (new_start - old_start) * BX


def pack_kernel(
    sub_count, old_hbm, new_hbm, pop_ref, one_ref, two_ref, far_ref, all_ref, info_ref, old_ref, new_ref, sem,
):
    curve, sub = lax.axis_index("curve"), lax.axis_index("sub")
    counts = [
        pltpu.make_async_copy(source, target, sem.at[at])
        for at, (source, target) in enumerate(((old_hbm, old_ref), (new_hbm, new_ref)))
    ]
    loads = [
        pltpu.make_async_copy(
            pop_ref.at[:, :, half * LANES : (half + 1) * LANES], all_ref.at[:, half], sem.at[2 + half]
        )
        for half in range(HALVES)
    ]
    for load in counts + loads:
        load.start()
    for load in counts:
        load.wait()
    held_old, held_new, offset = layout_of(sub_count, old_ref, new_ref, curve, sub)
    info_ref[0] = held_old
    info_ref[1] = held_new
    info_ref[2] = offset
    for load in loads:
        load.wait()
    even = sub % 2 == 0
    right = held_old - REACH
    one_start = jnp.where(even, right, 0)
    two_start = jnp.where(even, 0, right)
    far_start = jnp.where(sub == 0, 0, held_old - STEPS)
    for target, start, count in (
        (one_ref, one_start, REACH),
        (two_ref, two_start, REACH),
        (far_ref, far_start, STEPS),
    ):
        for direction in range(DIRS):
            for half in range(HALVES):
                row = (direction * HALVES + half) * count
                target[row : row + count, :] = all_ref[direction, half, pl.ds(start, count), :]


def fetch(source, row, moved):
    return [
        [source[direction, half, pl.ds(row - int(VELOCITY[direction, 0]) * moved, 8), :] for direction in range(DIRS)]
        for half in range(HALVES)
    ]


def shift(halves, tables):
    moved = [shift_cross(halves[0][direction], halves[1][direction], direction, tables) for direction in range(DIRS)]
    return [[pair[half] for pair in moved] for half in range(HALVES)]


def store(target, row, halves):
    for half in range(HALVES):
        for direction in range(DIRS):
            target[direction, half, pl.ds(row, 8), :] = halves[half][direction]


def inner_kernel(
    slots, info_ref, first_ref, out_ref, own_ref, cross_ref, edge_ref,
    ping_ref, pong_ref, raw_ref, tile_ref, zero_ref, out_sem,
):
    held_old, held_new, offset = info_ref[0], info_ref[1], info_ref[2]
    end = offset + held_new

    def clear(slot):
        return pltpu.make_async_copy(
            zero_ref, out_ref.at[:, slot * BX : (slot + 1) * BX, :], out_sem.at[slot]
        )

    @pl.when(held_new < slots * BX)
    def _():
        zero_ref[...] = jnp.zeros_like(zero_ref)

    for slot in range(slots):

        @pl.when(slot * BX >= held_new)
        def _():
            clear(slot).start()

    for direction in range(DIRS):
        for half in range(HALVES):
            own_ref[direction, half, :STEPS, :] = first_ref[direction, half, :STEPS, :]
            own_ref[direction, half, STEPS:, :] = first_ref[direction, half, pl.ds(held_old - STEPS, STEPS), :]
    tables = moves()
    last = held_old - STEPS - 1 + PAD
    pairs = held_old // 16

    def run(step, source, target):
        def settle(row):
            waiting = [fetch(raw_ref, at, 0) for at in (0, 8)]
            return [shift(halves, tables) for halves in waiting], (row, row + 8)

        def body(pair, carry):
            row = pl.multiple_of(pair * 16, 16)
            top = row if step == 0 else row + PAD
            values, rows = settle(pl.multiple_of(PAD + 16 * jnp.maximum(pair - 1, 0), 8))
            cells = [fetch(source, at, 1 if step else 0) for at in (top, top + 8)]
            relaxed = [[collide(half) for half in halves] for halves in cells]
            for at, halves in zip(rows, values):
                store(target, at, halves)
            for at, halves in zip((0, 8), relaxed):
                store(raw_ref, at, halves)
            return carry

        lax.fori_loop(0, pairs, body, 0)
        values, rows = settle(pl.multiple_of(PAD + 16 * (pairs - 1), 8))
        for at, halves in zip(rows, values):
            store(target, at, halves)
        for side, first in ((0, 6), (1, 1)):
            for at in range(5):
                for half in range(HALVES):
                    row = last if side else PAD + STEPS
                    cross_ref[((step * 2 + side) * 5 + at) * HALVES + half, :] = target[
                        first + at, half, row, :
                    ]

    run(0, first_ref, ping_ref)
    run(1, ping_ref, pong_ref)
    run(2, pong_ref, ping_ref)
    run(3, ping_ref, pong_ref)

    tiles = slots * BX // 8

    def write(tile):
        row = pl.multiple_of(jnp.clip(tile * 8 - offset, 0, (tiles - 1) * 8), 8)
        return pltpu.make_async_copy(
            tile_ref.at[:, tile * 8 : tile * 8 + 8, :], out_ref.at[:, pl.ds(row, 8), :], out_sem.at[slots + tile]
        )

    def kept(tile):
        inside = jnp.logical_and(tile * 8 >= offset, tile * 8 < end)
        return jnp.logical_and(inside, tile * 8 < held_old - 8)

    for tile in range(tiles):

        @pl.when(tile * 8 < held_old)
        def _():
            halves = fetch(pong_ref, PAD + tile * 8, 1)
            for direction in range(DIRS):
                for half in range(HALVES):
                    lanes = slice(half * LANES, (half + 1) * LANES)
                    tile_ref[direction, tile * 8 : tile * 8 + 8, lanes] = halves[half][direction]

        if tile > 0:

            @pl.when(kept(tile))
            def _():
                write(tile).start()

    right = pl.multiple_of(held_old - 8, 8)
    for direction in range(DIRS):
        edge_ref[direction, 0:8, :] = tile_ref[direction, 0:8, :]
        edge_ref[direction, 8:16, :] = tile_ref[direction, pl.ds(right, 8), :]
    for slot in range(slots):

        @pl.when(slot * BX >= held_new)
        def _():
            clear(slot).wait()

    for tile in range(1, tiles):

        @pl.when(kept(tile))
        def _():
            write(tile).wait()


def edge_kernel(sub_count, inside, info_ref, own_ref, cross_ref, edge_ref, *refs):
    if inside:
        near_ref, far_ref, (_, out_ref, strip_ref, done_ref, sem) = refs[0], None, refs[1:]
    else:
        near_ref, far_ref, _, out_ref, strip_ref, done_ref, sem = refs
    sub = lax.axis_index("sub")
    held_old, held_new, offset = info_ref[0], info_ref[1], info_ref[2]
    gained = offset + held_new - held_old
    even = sub % 2 == 0
    on_right = even if inside else jnp.logical_not(even)
    on_left = jnp.logical_not(on_right)
    extra = jnp.where(on_right, gained, -offset)
    heavy, light = extra > 0, extra == 0

    def place(source, count, first, used, start):
        for direction in range(DIRS):
            for half in range(HALVES):
                row = (direction * HALVES + half) * count + first
                strip_ref[0, direction, half, start : start + used, :] = source[row : row + used, :]

    def both(first, second):
        return jnp.logical_and(first, second)

    if far_ref is None:
        local = light
    else:
        outer = jnp.logical_or(sub == 0, sub == sub_count - 1)
        local = both(light, jnp.logical_not(outer))

        @pl.when(both(outer, on_left))
        def _():
            place(far_ref, STEPS, 0, STEPS, LEFT_EDGE - 2 * STEPS)

        @pl.when(both(outer, on_right))
        def _():
            place(far_ref, STEPS, 0, STEPS, PAD + STEPS)

    @pl.when(both(local, on_left))
    def _():
        place(near_ref, REACH, REACH - STEPS, STEPS, LEFT_EDGE - 2 * STEPS)

    @pl.when(both(local, on_right))
    def _():
        place(near_ref, REACH, 0, STEPS, PAD + STEPS)

    @pl.when(both(heavy, on_left))
    def _():
        place(near_ref, REACH, 0, REACH, PAD)

    @pl.when(both(heavy, on_right))
    def _():
        place(near_ref, REACH, 0, REACH, PAD + STEPS)

    @pl.when(on_left)
    def _():
        for direction in range(DIRS):
            for half in range(HALVES):
                strip_ref[0, direction, half, LEFT_EDGE - STEPS : LEFT_EDGE, :] = own_ref[direction, half, :STEPS, :]

    @pl.when(on_right)
    def _():
        for direction in range(DIRS):
            for half in range(HALVES):
                strip_ref[0, direction, half, PAD : PAD + STEPS, :] = own_ref[direction, half, STEPS:, :]

    for side, first, row, here in ((0, 6, LEFT_EDGE, on_left), (1, 1, PAD - 1, on_right)):

        @pl.when(here)
        def _():
            for step in range(STEPS):
                for at in range(5):
                    for half in range(HALVES):
                        strip_ref[step + 1, first + at, half, row, :] = cross_ref[
                            ((step * 2 + side) * 5 + at) * HALVES + half, :
                        ]

    tables = moves()

    def run(rows):
        def body(step, carry):
            moved = jnp.minimum(step, 1)
            cells = [fetch(strip_ref.at[step], row, moved) for row in rows]
            relaxed = [shift([collide(half) for half in halves], tables) for halves in cells]
            for row, halves in zip(rows, relaxed):
                store(strip_ref.at[step + 1], row, halves)
            return carry

        lax.fori_loop(0, STEPS, body, 0)

    @pl.when(heavy)
    def _():
        run([PAD, PAD + 8, PAD + 16])

    @pl.when(light)
    def _():
        run([pl.multiple_of(jnp.where(on_left, PAD + 16, PAD), 8)])

    final = strip_ref.at[STEPS]
    plane = lax.broadcasted_iota(jnp.int32, (8, LANES), 0)

    def finish(side, merged, whole, row):
        for at, start in [merged] + whole:
            halves = fetch(final, start, 1)
            for direction in range(DIRS):
                for half in range(HALVES):
                    lanes = slice(half * LANES, (half + 1) * LANES)
                    value = halves[half][direction]
                    if (at, start) == merged:
                        mine = plane < STEPS if side == 0 else plane >= STEPS
                        value = jnp.where(mine, value, edge_ref[direction, side * 8 : side * 8 + 8, lanes])
                    done_ref[direction, at : at + 8, lanes] = value
        count = 8 + 8 * len(whole)
        low = min(at for at, _ in [merged] + whole)
        copy = pltpu.make_async_copy(
            done_ref.at[:, low : low + count, :], out_ref.at[:, pl.ds(pl.multiple_of(row, 8), count), :], sem
        )
        copy.start()
        copy.wait()

    low, high = LEFT_EDGE - STEPS, PAD - STEPS
    edge_row = held_old - 8 - offset

    @pl.when(both(heavy, on_left))
    def _():
        finish(0, (16, low), [(0, low - 16), (8, low - 8)], 0)

    @pl.when(both(light, on_left))
    def _():
        finish(0, (16, low), [], 0)

    @pl.when(both(heavy, on_right))
    def _():
        finish(1, (0, high), [(8, high + 8), (16, high + 16)], edge_row)

    @pl.when(both(light, on_right))
    def _():
        finish(1, (0, high), [], edge_row)


def shards(populations, count_old, count_new):
    curve_count, sub_count = lax.axis_size("curve"), lax.axis_size("sub")
    planes = populations.shape[1]
    slots = planes // BX
    total = curve_count * sub_count
    old, new = count_old.T, count_new.T
    smem = pl.BlockSpec(memory_space=pltpu.SMEM)
    hbm = pl.BlockSpec(memory_space=pltpu.HBM)
    vmem = pl.BlockSpec(memory_space=pltpu.VMEM)
    rows = DIRS * HALVES
    whole = jax.ShapeDtypeStruct(populations.shape, jnp.float32)

    def local(*shape):
        return pltpu.VMEM(shape, jnp.float32)

    def near(value):
        return pltpu.with_memory_space_constraint(value, pltpu.VMEM)

    params = pltpu.CompilerParams(vmem_limit_bytes=32 << 20)
    populations, old, new = (
        pltpu.with_memory_space_constraint(value, pltpu.HBM) for value in (populations, old, new)
    )
    one, two, rim, cells, info = pl.pallas_call(
        functools.partial(pack_kernel, sub_count),
        out_shape=(
            local(rows * REACH, LANES),
            local(rows * REACH, LANES),
            local(rows * STEPS, LANES),
            local(DIRS, HALVES, planes, LANES),
            pltpu.SMEM((4,), jnp.int32),
        ),
        in_specs=[hbm, hbm, hbm],
        out_specs=(vmem, vmem, vmem, vmem, smem),
        scratch_shapes=[
            pltpu.SMEM(old.shape, jnp.int32),
            pltpu.SMEM(old.shape, jnp.int32),
            pltpu.SemaphoreType.DMA((2 + HALVES,)),
        ],
        compiler_params=params,
        name="pack",
    )(old, new, populations)
    info = pltpu.with_memory_space_constraint(info, pltpu.SMEM)
    cells = near(cells)
    both = ("curve", "sub")

    def everyone(pairs):
        busy = {source for source, _ in pairs}
        rest = [at for at in range(total) if at not in busy]
        return pairs + [(at, (at // sub_count ^ 1) * sub_count + at % sub_count) for at in rest]

    inside = [(at, at ^ 1) for at in range(total)]
    between, across = [], []
    for at in range(1, total, 2):
        after = (at + 1) % total
        into = across if after % sub_count == 0 else between
        into += [(at, after), (after, at)]
    one = lax.ppermute(one, both, inside)
    two = lax.ppermute(two, both, everyone(between))
    rim = lax.ppermute(rim, both, everyone(across))
    state = pltpu.VMEM((DIRS, HALVES, planes + 2 * PAD, LANES), jnp.float32)
    result, own, cross, edge = pl.pallas_call(
        functools.partial(inner_kernel, slots),
        out_shape=(
            whole,
            local(DIRS, HALVES, 2 * STEPS, LANES),
            local(STEPS * 2 * 5 * HALVES, LANES),
            local(DIRS, 16, HALVES * LANES),
        ),
        in_specs=[smem, vmem],
        out_specs=(hbm, vmem, vmem, vmem),
        scratch_shapes=[
            state,
            state,
            pltpu.VMEM((DIRS, HALVES, 16, LANES), jnp.float32),
            pltpu.VMEM(populations.shape, jnp.float32),
            pltpu.VMEM((DIRS, BX, HALVES * LANES), jnp.float32),
            pltpu.SemaphoreType.DMA((slots + slots * BX // 8,)),
        ],
        compiler_params=params,
        cost_estimate=pl.CostEstimate(flops=10**9, bytes_accessed=8 * 10**6, transcendentals=0),
        name="inner",
    )(info, cells)
    own, cross, edge = near(own), near(cross), near(edge)
    for at, received in enumerate(((one,), (two, rim))):
        result = pl.pallas_call(
            functools.partial(edge_kernel, sub_count, at == 0),
            out_shape=whole,
            in_specs=[smem, vmem, vmem, vmem] + [vmem] * len(received) + [hbm],
            out_specs=hbm,
            scratch_shapes=[
                pltpu.VMEM((STEPS + 1, DIRS, HALVES, STRIP, LANES), jnp.float32),
                pltpu.VMEM((DIRS, 24, HALVES * LANES), jnp.float32),
                pltpu.SemaphoreType.DMA,
            ],
            input_output_aliases={4 + len(received): 0},
            compiler_params=params,
            cost_estimate=pl.CostEstimate(flops=10**8, bytes_accessed=10**6, transcendentals=0),
            name="edges",
        )(info, own, cross, edge, *map(near, received), result)
    return result


def solution(mesh):
    if mesh.shape["sub"] % 2 or mesh.shape["curve"] % 2:
        raise ValueError("odd mesh")
    in_specs = (P(None, ("curve", "sub"), None), P(), P())
    out_specs = P(None, ("curve", "sub"), None)
    return jax.shard_map(shards, mesh=mesh, in_specs=in_specs, out_specs=out_specs, check_vma=False)
```

profile of v0, /device:TPU:0, one launch (start us, length us, event | category | flops | bytes accessed | tf_op | source)
XLA Modules:
  0.0 19.7 jit_solution(7812676682915245265)
XLA Ops:
  0.0 1.4 %pack.1 = (f32[760,128]{1,0:T(8,128)S(1)}, f32[760,128]{1,0:T(8,128)S(1)}, f32[152,128]{1,0:T(8,128)S(1)}, f32[19,2,64,128]{3,2,1,0:T(8,128)S(1)}, s32[4]{0:T(128)S(4)}) custom-call(s32[4,8]{1,0:T(4,128)} %bitcast.2, s32[4,8]{1,0:T(4,128)} %bitcast.3, f32[19,64,256]{2,1,0:T(8,128)} %pop_ref.1), custom_call_target="tpu_custom_call" | custom-call | tf_op jit(solution)/shard_map/pack/pallas_call | solution.py:491
  1.4 3.1 %collective-permute-start.2 = (f32[760,128]{1,0:T(8,128)S(1)}, f32[760,128]{1,0:T(8,128)S(1)}, u32[]{:S(2)}, u32[]{:S(2)}) collective-permute-start(f32[760,128]{1,0:T(8,128)S(1)} %get-tuple-element.21), channel_id=1, source_target_pairs={{0,1},{1,0},{2,3},{3,2},{4,5},{5,4},{6,7},{7,6},{8,9},{9,8},{10,11... | collective-permute-start | bytes 1167368 | tf_op jit(solution)/shard_map/ppermute | solution.py:525
  4.5 0.0 collective-permute-start
  4.5 4.5 %collective-permute-start.1 = (f32[152,128]{1,0:T(8,128)S(1)}, f32[152,128]{1,0:T(8,128)S(1)}, u32[]{:S(2)}, u32[]{:S(2)}) collective-permute-start(f32[152,128]{1,0:T(8,128)S(1)} %get-tuple-element.20), channel_id=1, source_target_pairs={{3,4},{4,3},{7,8},{8,7},{11,12},{12,11},{15,16},{16,15},{19,20},{2... | collective-permute-start | bytes 233480 | tf_op jit(solution)/shard_map/ppermute | solution.py:527
  9.0 4.3 %inner.1 = (f32[19,64,256]{2,1,0:T(8,128)}, f32[19,2,8,128]{3,2,1,0:T(8,128)S(1)}, f32[80,128]{1,0:T(8,128)S(1)}, f32[19,16,256]{2,1,0:T(8,128)S(1)}) custom-call(s32[4]{0:T(128)S(4)} %get-tuple-element.14.info_ref, f32[19,2,64,128]{3,2,1,0:T(8,128)S(1)} %get-tuple-element.15.first_ref), custom_call_target="tpu_custom_call" | custom-call | flops 1000000000 | bytes 8000000 | tf_op jit(solution)/shard_map/inner/pallas_call | solution.py:529
  13.4 0.3 %collective-permute-done.2.refs_0_ = f32[760,128]{1,0:T(8,128)S(1)} collective-permute-done((f32[760,128]{1,0:T(8,128)S(1)}, f32[760,128]{1,0:T(8,128)S(1)}, u32[]{:S(2)}, u32[]{:S(2)}) %collective-permute-start.2) | collective-permute-done | bytes 389152 | tf_op jit(solution)/shard_map/ppermute | solution.py:525
  13.7 1.5 %edges.2.refs_2_ = f32[19,64,256]{2,1,0:T(8,128)} custom-call(s32[4]{0:T(128)S(4)} %get-tuple-element.14.info_ref, f32[19,2,8,128]{3,2,1,0:T(8,128)S(1)} %get-tuple-element.16.own_ref, f32[80,128]{1,0:T(8,128)S(1)} %get-tuple-element.17.cross_ref, f32[19,16,256]{2,1,0:T(8,128)S(1)} %get-tuple-element.18.edge_ref, ...), custom_call_target="tpu_custom_call", output_to_operand_aliasing={{}: (5, {})} | custom-call | flops 100000000 | bytes 1000000 | tf_op jit(solution)/shard_map/edges/pallas_call | solution.py:553
  15.2 3.0 %collective-permute-done.1.refs_1_ = f32[152,128]{1,0:T(8,128)S(1)} collective-permute-done((f32[152,128]{1,0:T(8,128)S(1)}, f32[152,128]{1,0:T(8,128)S(1)}, u32[]{:S(2)}, u32[]{:S(2)}) %collective-permute-start.1) | collective-permute-done | bytes 77856 | tf_op jit(solution)/shard_map/ppermute | solution.py:527
  18.2 0.0 collective-permute-done.refs_0_
  18.2 1.5 %edges.3 = f32[19,64,256]{2,1,0:T(8,128)} custom-call(s32[4]{0:T(128)S(4)} %get-tuple-element.14.info_ref, f32[19,2,8,128]{3,2,1,0:T(8,128)S(1)} %get-tuple-element.16.own_ref, f32[80,128]{1,0:T(8,128)S(1)} %get-tuple-element.17.cross_ref, f32[19,16,256]{2,1,0:T(8,128)S(1)} %get-tuple-element.18.edge_ref, ...), custom_call_target="tpu_custom_call", output_to_operand_aliasing={{}: (6, {})} | custom-call | flops 100000000 | bytes 1000000 | tf_op jit(solution)/shard_map/edges/pallas_call | solution.py:553
Async XLA Ops:
  1.4 12.2 %collective-permute-start.2 = (f32[760,128]{1,0:T(8,128)S(1)}, f32[760,128]{1,0:T(8,128)S(1)}, u32[]{:S(2)}, u32[]{:S(2)}) collective-permute-start(f32[760,128]{1,0:T(8,128)S(1)} %get-tuple-element.21), channel_id=1, source_target_pairs={{0,1},{1,0},{2,3},{3,2},{4,5},{5,4},{6,7},{7,6},{8,9},{9,8},{10,11... | collective-permute-start | bytes 1167368 | tf_op jit(solution)/shard_map/ppermute | solution.py:525
  4.5 13.6 %collective-permute-start = (f32[760,128]{1,0:T(8,128)S(1)}, f32[760,128]{1,0:T(8,128)S(1)}, u32[]{:S(2)}, u32[]{:S(2)}) collective-permute-start(f32[760,128]{1,0:T(8,128)S(1)} %get-tuple-element.19), channel_id=1, source_target_pairs={{1,2},{2,1},{5,6},{6,5},{9,10},{10,9},{13,14},{14,13},{17,18},{18,... | collective-permute-start | bytes 1167368 | tf_op jit(solution)/shard_map/ppermute | solution.py:526
  4.5 13.6 %collective-permute-start.1 = (f32[152,128]{1,0:T(8,128)S(1)}, f32[152,128]{1,0:T(8,128)S(1)}, u32[]{:S(2)}, u32[]{:S(2)}) collective-permute-start(f32[152,128]{1,0:T(8,128)S(1)} %get-tuple-element.20), channel_id=1, source_target_pairs={{3,4},{4,3},{7,8},{8,7},{11,12},{12,11},{15,16},{16,15},{19,20},{2... | collective-permute-start | bytes 233480 | tf_op jit(solution)/shard_map/ppermute | solution.py:527
where the time goes:
time: 19.9 us; the launch traced here: 19.7 us
  Pallas kernels  8.82 us (44%)
  starting transfers between devices  7.59 us (38%)
  waiting for transfers between devices  3.27 us (16%)
    ppermute x1, starting transfers between devices, shards(): rim = lax.ppermute(rim, both, everyone(across))  4.47 us
    pallas_call x1, Pallas kernels, shards(): pl.pallas_call(functools.partial(inner_kernel, slots), out_shape=(whole,...  4.35 us
    ppermute x1, starting transfers between devices, shards(): one = lax.ppermute(one, both, inside)  3.12 us
    pallas_call x2, Pallas kernels, shards(): pl.pallas_call(functools.partial(edge_kernel, sub_count, at == 0), out_sh...  3.07 us
    ppermute x1, waiting for transfers between devices, shards(): rim = lax.ppermute(rim, both, everyone(across))  2.98 us
    pallas_call x1, Pallas kernels, shards(): pl.pallas_call(functools.partial(pack_kernel, sub_count), out_shape=(loca...  1.41 us
  transfers between devices with their start and end apart: 3, of which 2 were waited for; matrix products, arithmetic and copies ran while one was open for 0% of the time, Pallas kernels for 30%

commit v1 on v0

--- a/solution.py
+++ b/solution.py
@@ -16,8 +16,11 @@
 LANES = 128
 HALVES = 2
 PAD = 8
-STRIP = 40
-LEFT_EDGE = 32
+STRIP = 72
+MID = 32
+SPLIT = 10
+TOWARD = {0: (6, 7, 8, 9, 10), 1: (1, 2, 3, 4, 5)}
+LEVEL = (0, 11, 12, 13, 14, 15, 16, 17, 18)
 
 VELOCITY = np.array(
     [
@@ -161,7 +164,7 @@
 
 
 def pack_kernel(
-    sub_count, old_hbm, new_hbm, pop_ref, one_ref, two_ref, far_ref, all_ref, info_ref, old_ref, new_ref, sem,
+    sub_count, old_hbm, new_hbm, pop_ref, one_ref, more_ref, two_ref, all_ref, info_ref, old_ref, new_ref, sem,
 ):
     curve, sub = lax.axis_index("curve"), lax.axis_index("sub")
     counts = [
@@ -188,11 +191,10 @@
     right = held_old - REACH
     one_start = jnp.where(even, right, 0)
     two_start = jnp.where(even, 0, right)
-    far_start = jnp.where(sub == 0, 0, held_old - STEPS)
     for target, start, count in (
-        (one_ref, one_start, REACH),
+        (one_ref, one_start, SPLIT),
+        (more_ref, one_start + SPLIT, REACH - SPLIT),
         (two_ref, two_start, REACH),
-        (far_ref, far_start, STEPS),
     ):
         for direction in range(DIRS):
             for half in range(HALVES):
@@ -218,8 +220,40 @@
             target[direction, half, pl.ds(row, 8), :] = halves[half][direction]
 
 
+def rim_parts(side):
+    parts, row = [], 0
+    for half in range(HALVES):
+        for directions, count in ((TOWARD[side], 4), (LEVEL, 3), (TOWARD[1 - side], 2)):
+            for direction in directions:
+                parts.append((direction, half, row, 0 if side == 0 else STEPS - count, count))
+                row += count
+    return parts
+
+
+RIM = sum(part[-1] for part in rim_parts(0))
+
+
+def rim_kernel(sub_count, info_ref, cells_ref, far_ref):
+    sub = lax.axis_index("sub")
+    tables = moves()
+
+    def send(side, row):
+        relaxed = shift([collide(half) for half in fetch(cells_ref, row, 0)], tables)
+        for direction, half, at, first, count in rim_parts(side):
+            first += STEPS * side
+            far_ref[at : at + count, :] = relaxed[half][direction][first : first + count, :]
+
+    @pl.when(sub == 0)
+    def _():
+        send(0, 0)
+
+    @pl.when(sub == sub_count - 1)
+    def _():
+        send(1, pl.multiple_of(info_ref[0] - 8, 8))
+
+
 def inner_kernel(
-    slots, info_ref, first_ref, out_ref, own_ref, cross_ref, edge_ref,
+    slots, info_ref, first_ref, out_ref, own_ref, next_ref, cross_ref, edge_ref,
     ping_ref, pong_ref, raw_ref, tile_ref, zero_ref, out_sem,
 ):
     held_old, held_new, offset = info_ref[0], info_ref[1], info_ref[2]
@@ -278,6 +312,10 @@
                     ]
 
     run(0, first_ref, ping_ref)
+    for direction in range(DIRS):
+        for half in range(HALVES):
+            next_ref[direction, half, :STEPS, :] = ping_ref[direction, half, PAD : PAD + STEPS, :]
+            next_ref[direction, half, STEPS:, :] = ping_ref[direction, half, pl.ds(last + 1, STEPS), :]
     run(1, ping_ref, pong_ref)
     run(2, pong_ref, ping_ref)
     run(3, ping_ref, pong_ref)
@@ -327,19 +365,84 @@
             write(tile).wait()
 
 
-def edge_kernel(sub_count, inside, info_ref, own_ref, cross_ref, edge_ref, *refs):
-    if inside:
-        near_ref, far_ref, (_, out_ref, strip_ref, done_ref, sem) = refs[0], None, refs[1:]
-    else:
-        near_ref, far_ref, _, out_ref, strip_ref, done_ref, sem = refs
+def both(first, second):
+    return jnp.logical_and(first, second)
+
+
+def finish(side, source, merged, whole, row, edge_ref, out_ref, done_ref, sem):
+    plane = lax.broadcasted_iota(jnp.int32, (8, LANES), 0)
+    mine = plane < STEPS if side == 0 else plane >= STEPS
+    for at, start in [merged] + whole:
+        halves = fetch(source, start, 1)
+        for direction in range(DIRS):
+            for half in range(HALVES):
+                lanes = slice(half * LANES, (half + 1) * LANES)
+                value = halves[half][direction]
+                if (at, start) == merged:
+                    value = jnp.where(mine, value, edge_ref[direction, side * 8 : side * 8 + 8, lanes])
+                done_ref[direction, at : at + 8, lanes] = value
+    low, count = min(at for at, _ in [merged] + whole), 8 + 8 * len(whole)
+    copy = pltpu.make_async_copy(
+        done_ref.at[:, low : low + count, :], out_ref.at[:, pl.ds(pl.multiple_of(row, 8), count), :], sem
+    )
+    copy.start()
+    return copy
+
+
+def outer_kernel(
+    sub_count, info_ref, next_ref, cross_ref, edge_ref, far_ref, _, out_ref, strip_ref, done_ref, sem,
+):
+    sub = lax.axis_index("sub")
+    held_old, offset = info_ref[0], info_ref[2]
+
+    def end(side):
+        beside, own, border = (PAD, PAD + STEPS, PAD + 8) if side == 0 else (PAD + STEPS, PAD, PAD - 1)
+        for direction, half, at, first, count in rim_parts(1 - side):
+            strip_ref[0, direction, half, beside + first : beside + first + count, :] = far_ref[at : at + count, :]
+        for direction in range(DIRS):
+            for half in range(HALVES):
+                strip_ref[0, direction, half, own : own + STEPS, :] = next_ref[
+                    direction, half, side * STEPS : (side + 1) * STEPS, :
+                ]
+        for step in range(STEPS):
+            for at in range(5):
+                for half in range(HALVES):
+                    strip_ref[step, TOWARD[side][at], half, border, :] = cross_ref[
+                        ((step * 2 + side) * 5 + at) * HALVES + half, :
+                    ]
+        tables = moves()
+
+        def body(step, carry):
+            relaxed = shift([collide(half) for half in fetch(strip_ref.at[step], PAD, 1)], tables)
+            store(strip_ref.at[step + 1], PAD, relaxed)
+            return carry
+
+        lax.fori_loop(0, STEPS - 1, body, 0)
+        start, row = (PAD + STEPS, 0) if side == 0 else (PAD - STEPS, held_old - 8 - offset)
+        finish(side, strip_ref.at[STEPS - 1], (0, start), [], row, edge_ref, out_ref, done_ref, sem).wait()
+
+    @pl.when(sub == 0)
+    def _():
+        end(0)
+
+    @pl.when(sub == sub_count - 1)
+    def _():
+        end(1)
+
+
+def tail_kernel(
+    sub_count, info_ref, own_ref, cross_ref, edge_ref, one_ref, more_ref, two_ref, _, out_ref,
+    strip_ref, left_ref, right_ref, sem,
+):
     sub = lax.axis_index("sub")
     held_old, held_new, offset = info_ref[0], info_ref[1], info_ref[2]
     gained = offset + held_new - held_old
+    lefts = jnp.where(offset == 0, 1, jnp.where(offset < 0, 3, 0))
+    rights = jnp.where(gained == 0, 1, jnp.where(gained > 0, 3, 0))
+    lefts = jnp.where(sub == 0, 0, lefts)
+    rights = jnp.where(sub == sub_count - 1, 0, rights)
     even = sub % 2 == 0
-    on_right = even if inside else jnp.logical_not(even)
-    on_left = jnp.logical_not(on_right)
-    extra = jnp.where(on_right, gained, -offset)
-    heavy, light = extra > 0, extra == 0
+    odd = jnp.logical_not(even)
 
     def place(source, count, first, used, start):
         for direction in range(DIRS):
@@ -347,123 +450,96 @@
                 row = (direction * HALVES + half) * count + first
                 strip_ref[0, direction, half, start : start + used, :] = source[row : row + used, :]
 
-    def both(first, second):
-        return jnp.logical_and(first, second)
-
-    if far_ref is None:
-        local = light
-    else:
-        outer = jnp.logical_or(sub == 0, sub == sub_count - 1)
-        local = both(light, jnp.logical_not(outer))
-
-        @pl.when(both(outer, on_left))
-        def _():
-            place(far_ref, STEPS, 0, STEPS, LEFT_EDGE - 2 * STEPS)
-
-        @pl.when(both(outer, on_right))
-        def _():
-            place(far_ref, STEPS, 0, STEPS, PAD + STEPS)
-
-    @pl.when(both(local, on_left))
-    def _():
-        place(near_ref, REACH, REACH - STEPS, STEPS, LEFT_EDGE - 2 * STEPS)
-
-    @pl.when(both(local, on_right))
-    def _():
-        place(near_ref, REACH, 0, STEPS, PAD + STEPS)
-
-    @pl.when(both(heavy, on_left))
-    def _():
-        place(near_ref, REACH, 0, REACH, PAD)
-
-    @pl.when(both(heavy, on_right))
-    def _():
-        place(near_ref, REACH, 0, REACH, PAD + STEPS)
-
-    @pl.when(on_left)
-    def _():
-        for direction in range(DIRS):
-            for half in range(HALVES):
-                strip_ref[0, direction, half, LEFT_EDGE - STEPS : LEFT_EDGE, :] = own_ref[direction, half, :STEPS, :]
-
-    @pl.when(on_right)
-    def _():
-        for direction in range(DIRS):
-            for half in range(HALVES):
-                strip_ref[0, direction, half, PAD : PAD + STEPS, :] = own_ref[direction, half, STEPS:, :]
-
-    for side, first, row, here in ((0, 6, LEFT_EDGE, on_left), (1, 1, PAD - 1, on_right)):
-
-        @pl.when(here)
-        def _():
+    low, high, rest = MID - STEPS - REACH, MID + 8 + STEPS, REACH - SPLIT
+
+    for here, count, start, light in ((odd, lefts, low, False), (even, rights, high, True)):
+
+        @pl.when(both(here, count == 3))
+        def _():
+            place(one_ref, SPLIT, 0, SPLIT, start)
+            place(more_ref, rest, 0, rest, start + SPLIT)
+
+        @pl.when(both(here, count == 1))
+        def _():
+            if light:
+                place(one_ref, SPLIT, 0, STEPS, start)
+            else:
+                place(more_ref, rest, rest - STEPS, STEPS, start + REACH - STEPS)
+
+    for here, count, start, first in ((even, lefts, low, REACH - STEPS), (odd, rights, high, 0)):
+
+        @pl.when(both(here, count == 3))
+        def _():
+            place(two_ref, REACH, 0, REACH, start)
+
+        @pl.when(both(here, count == 1))
+        def _():
+            place(two_ref, REACH, first, STEPS, start + first)
+
+    for side, count, start, border in ((0, lefts, MID - STEPS, MID), (1, rights, MID + 8, MID + 7)):
+
+        @pl.when(count > 0)
+        def _():
+            for direction in range(DIRS):
+                for half in range(HALVES):
+                    strip_ref[0, direction, half, start : start + STEPS, :] = own_ref[
+                        direction, half, side * STEPS : (side + 1) * STEPS, :
+                    ]
             for step in range(STEPS):
                 for at in range(5):
                     for half in range(HALVES):
-                        strip_ref[step + 1, first + at, half, row, :] = cross_ref[
+                        strip_ref[step + 1, TOWARD[side][at], half, border, :] = cross_ref[
                             ((step * 2 + side) * 5 + at) * HALVES + half, :
                         ]
 
     tables = moves()
-
-    def run(rows):
-        def body(step, carry):
-            moved = jnp.minimum(step, 1)
-            cells = [fetch(strip_ref.at[step], row, moved) for row in rows]
-            relaxed = [shift([collide(half) for half in halves], tables) for halves in cells]
-            for row, halves in zip(rows, relaxed):
-                store(strip_ref.at[step + 1], row, halves)
-            return carry
-
-        lax.fori_loop(0, STEPS, body, 0)
-
-    @pl.when(heavy)
-    def _():
-        run([PAD, PAD + 8, PAD + 16])
-
-    @pl.when(light)
-    def _():
-        run([pl.multiple_of(jnp.where(on_left, PAD + 16, PAD), 8)])
+    work = lefts + rights
+
+    def row_of(at):
+        return pl.multiple_of(jnp.where(at < lefts, MID - 8 * (lefts - at), MID + 8 + 8 * (at - lefts)), 8)
+
+    for groups in (1, 2, 3, 4, 6):
+
+        @pl.when(work == groups)
+        def _():
+            rows = [row_of(at) for at in range(groups)]
+
+            def body(step, carry):
+                moved = jnp.minimum(step, 1)
+                cells = [fetch(strip_ref.at[step], row, moved) for row in rows]
+                relaxed = [shift([collide(half) for half in halves], tables) for halves in cells]
+                for row, halves in zip(rows, relaxed):
+                    store(strip_ref.at[step + 1], row, halves)
+                return carry
+
+            lax.fori_loop(0, STEPS, body, 0)
 
     final = strip_ref.at[STEPS]
-    plane = lax.broadcasted_iota(jnp.int32, (8, LANES), 0)
-
-    def finish(side, merged, whole, row):
-        for at, start in [merged] + whole:
-            halves = fetch(final, start, 1)
-            for direction in range(DIRS):
-                for half in range(HALVES):
-                    lanes = slice(half * LANES, (half + 1) * LANES)
-                    value = halves[half][direction]
-                    if (at, start) == merged:
-                        mine = plane < STEPS if side == 0 else plane >= STEPS
-                        value = jnp.where(mine, value, edge_ref[direction, side * 8 : side * 8 + 8, lanes])
-                    done_ref[direction, at : at + 8, lanes] = value
-        count = 8 + 8 * len(whole)
-        low = min(at for at, _ in [merged] + whole)
-        copy = pltpu.make_async_copy(
-            done_ref.at[:, low : low + count, :], out_ref.at[:, pl.ds(pl.multiple_of(row, 8), count), :], sem
-        )
-        copy.start()
-        copy.wait()
-
-    low, high = LEFT_EDGE - STEPS, PAD - STEPS
-    edge_row = held_old - 8 - offset
-
-    @pl.when(both(heavy, on_left))
-    def _():
-        finish(0, (16, low), [(0, low - 16), (8, low - 8)], 0)
-
-    @pl.when(both(light, on_left))
-    def _():
-        finish(0, (16, low), [], 0)
-
-    @pl.when(both(heavy, on_right))
-    def _():
-        finish(1, (0, high), [(8, high + 8), (16, high + 16)], edge_row)
-
-    @pl.when(both(light, on_right))
-    def _():
-        finish(1, (0, high), [], edge_row)
+    first, last = MID - STEPS, MID + STEPS
+    row = held_old - 8 - offset
+    ends = (
+        (lefts, 0, (16, first), [(0, first - 16), (8, first - 8)], 0, left_ref),
+        (rights, 1, (0, last), [(8, last + 8), (16, last + 16)], row, right_ref),
+    )
+    for count, side, merged, whole, to, done in ends:
+        for amount, used in ((3, whole), (1, [])):
+
+            @pl.when(count == amount)
+            def _():
+                finish(side, final, merged, used, to, edge_ref, out_ref, done, sem.at[side])
+
+    for count, side, merged, whole, to, done in ends:
+        for amount in (3, 1):
+
+            @pl.when(count == amount)
+            def _():
+                size = 8 * amount
+                start = 0 if amount == 3 else merged[0]
+                pltpu.make_async_copy(
+                    done.at[:, start : start + size, :],
+                    out_ref.at[:, pl.ds(pl.multiple_of(to, 8), size), :],
+                    sem.at[side],
+                ).wait()
 
 
 def shards(populations, count_old, count_new):
@@ -488,12 +564,12 @@
     populations, old, new = (
         pltpu.with_memory_space_constraint(value, pltpu.HBM) for value in (populations, old, new)
     )
-    one, two, rim, cells, info = pl.pallas_call(
+    one, more, two, cells, info = pl.pallas_call(
         functools.partial(pack_kernel, sub_count),
         out_shape=(
+            local(rows * SPLIT, LANES),
+            local(rows * (REACH - SPLIT), LANES),
             local(rows * REACH, LANES),
-            local(rows * REACH, LANES),
-            local(rows * STEPS, LANES),
             local(DIRS, HALVES, planes, LANES),
             pltpu.SMEM((4,), jnp.int32),
         ),
@@ -509,12 +585,15 @@
     )(old, new, populations)
     info = pltpu.with_memory_space_constraint(info, pltpu.SMEM)
     cells = near(cells)
-    both = ("curve", "sub")
+    axes = ("curve", "sub")
 
     def everyone(pairs):
         busy = {source for source, _ in pairs}
         rest = [at for at in range(total) if at not in busy]
         return pairs + [(at, (at // sub_count ^ 1) * sub_count + at % sub_count) for at in rest]
+
+    def send(value, pairs):
+        return lax.ppermute(value, axes, pairs)
 
     inside = [(at, at ^ 1) for at in range(total)]
     between, across = [], []
@@ -522,20 +601,30 @@
         after = (at + 1) % total
         into = across if after % sub_count == 0 else between
         into += [(at, after), (after, at)]
-    one = lax.ppermute(one, both, inside)
-    two = lax.ppermute(two, both, everyone(between))
-    rim = lax.ppermute(rim, both, everyone(across))
+    one = send(one, inside)
+    two = send(two, everyone(between))
+    rim = pl.pallas_call(
+        functools.partial(rim_kernel, sub_count),
+        out_shape=local(RIM, LANES),
+        in_specs=[smem, vmem],
+        out_specs=vmem,
+        compiler_params=params,
+        name="rim",
+    )(info, cells)
+    rim = send(rim, everyone(across))
+    more = send(more, inside)
     state = pltpu.VMEM((DIRS, HALVES, planes + 2 * PAD, LANES), jnp.float32)
-    result, own, cross, edge = pl.pallas_call(
+    result, own, following, cross, edge = pl.pallas_call(
         functools.partial(inner_kernel, slots),
         out_shape=(
             whole,
+            local(DIRS, HALVES, 2 * STEPS, LANES),
             local(DIRS, HALVES, 2 * STEPS, LANES),
             local(STEPS * 2 * 5 * HALVES, LANES),
             local(DIRS, 16, HALVES * LANES),
         ),
         in_specs=[smem, vmem],
-        out_specs=(hbm, vmem, vmem, vmem),
+        out_specs=(hbm, vmem, vmem, vmem, vmem),
         scratch_shapes=[
             state,
             state,
@@ -548,24 +637,38 @@
         cost_estimate=pl.CostEstimate(flops=10**9, bytes_accessed=8 * 10**6, transcendentals=0),
         name="inner",
     )(info, cells)
-    own, cross, edge = near(own), near(cross), near(edge)
-    for at, received in enumerate(((one,), (two, rim))):
-        result = pl.pallas_call(
-            functools.partial(edge_kernel, sub_count, at == 0),
-            out_shape=whole,
-            in_specs=[smem, vmem, vmem, vmem] + [vmem] * len(received) + [hbm],
-            out_specs=hbm,
-            scratch_shapes=[
-                pltpu.VMEM((STEPS + 1, DIRS, HALVES, STRIP, LANES), jnp.float32),
-                pltpu.VMEM((DIRS, 24, HALVES * LANES), jnp.float32),
-                pltpu.SemaphoreType.DMA,
-            ],
-            input_output_aliases={4 + len(received): 0},
-            compiler_params=params,
-            cost_estimate=pl.CostEstimate(flops=10**8, bytes_accessed=10**6, transcendentals=0),
-            name="edges",
-        )(info, own, cross, edge, *map(near, received), result)
-    return result
+    own, following, cross, edge = map(near, (own, following, cross, edge))
+    result = pl.pallas_call(
+        functools.partial(outer_kernel, sub_count),
+        out_shape=whole,
+        in_specs=[smem, vmem, vmem, vmem, vmem, hbm],
+        out_specs=hbm,
+        scratch_shapes=[
+            pltpu.VMEM((STEPS, DIRS, HALVES, 3 * PAD, LANES), jnp.float32),
+            pltpu.VMEM((DIRS, 8, HALVES * LANES), jnp.float32),
+            pltpu.SemaphoreType.DMA,
+        ],
+        input_output_aliases={5: 0},
+        compiler_params=params,
+        cost_estimate=pl.CostEstimate(flops=10**8, bytes_accessed=10**6, transcendentals=0),
+        name="outer",
+    )(info, following, cross, edge, near(rim), result)
+    return pl.pallas_call(
+        functools.partial(tail_kernel, sub_count),
+        out_shape=whole,
+        in_specs=[smem] + [vmem] * 6 + [hbm],
+        out_specs=hbm,
+        scratch_shapes=[
+            pltpu.VMEM((STEPS + 1, DIRS, HALVES, STRIP, LANES), jnp.float32),
+            pltpu.VMEM((DIRS, 24, HALVES * LANES), jnp.float32),
+            pltpu.VMEM((DIRS, 24, HALVES * LANES), jnp.float32),
+            pltpu.SemaphoreType.DMA((2,)),
+        ],
+        input_output_aliases={7: 0},
+        compiler_params=params,
+        cost_estimate=pl.CostEstimate(flops=10**8, bytes_accessed=10**6, transcendentals=0),
+        name="tail",
+    )(info, own, cross, edge, near(one), near(more), near(two), result)
 
 
 def solution(mesh):

time: 19.9 us -> 22.4 us (1.13)
  starting transfers between devices: 7.59 us -> 8.67 us
  Pallas kernels: 8.82 us -> 9.64 us
  waiting for transfers between devices: 3.27 us -> 3.83 us
    ppermute x3 -> x4, starting transfers between devices: 7.59 us -> 8.67 us  [send(): return lax.ppermute(value, axes, pairs)]
    pallas_call x2 -> x3, Pallas kernels: 3.07 us -> 3.9 us  [the longest x1 2.39 us: shards(): pl.pallas_call(functools.partial(tail_kernel, sub_count), out_shape=whole...]
    ppermute x3 -> x4, waiting for transfers between devices: 3.27 us -> 3.83 us  [send(): return lax.ppermute(value, axes, pairs)]
  transfers between devices with their start and end apart: 3 -> 4, of which waited for: 2 -> 1; matrix products, arithmetic and copies ran while one was open for 0% -> 0% of each run, Pallas kernels for 30% -> 26%
where the time goes in v1:
time: 22.4 us; the launch traced here: 22.2 us
  Pallas kernels  9.64 us (43%)
  starting transfers between devices  8.67 us (39%)
  waiting for transfers between devices  3.83 us (17%)
    ppermute x4, starting transfers between devices, send(): return lax.ppermute(value, axes, pairs)  8.67 us
    pallas_call x1, Pallas kernels, shards(): pl.pallas_call(functools.partial(inner_kernel, slots), out_shape=(whole,...  4.34 us
    ppermute x4, waiting for transfers between devices, send(): return lax.ppermute(value, axes, pairs)  3.83 us
    pallas_call x1, Pallas kernels, shards(): pl.pallas_call(functools.partial(tail_kernel, sub_count), out_shape=whole...  2.39 us
    pallas_call x1, Pallas kernels, shards(): pl.pallas_call(functools.partial(pack_kernel, sub_count), out_shape=(loca...  1.4 us
    pallas_call x1, Pallas kernels, shards(): pl.pallas_call(functools.partial(outer_kernel, sub_count), out_shape=whol...  1.31 us
  transfers between devices with their start and end apart: 4, of which 1 were waited for; matrix products, arithmetic and copies ran while one was open for 0% of the time, Pallas kernels for 26%

profile of v1, /device:TPU:0, one launch (start us, length us, event | category | flops | bytes accessed | tf_op | source)
XLA Modules:
  0.0 22.2 jit_solution(2718335635782259882)
XLA Ops:
  0.0 1.4 %pack.1 = (f32[380,128]{1,0:T(8,128)S(1)}, f32[380,128]{1,0:T(8,128)S(1)}, f32[760,128]{1,0:T(8,128)S(1)}, f32[19,2,64,128]{3,2,1,0:T(8,128)S(1)}, s32[4]{0:T(128)S(4)}) custom-call(s32[4,8]{1,0:T(4,128)} %bitcast.2, s32[4,8]{1,0:T(4,128)} %bitcast.3, f32[19,64,256]{2,1,0:T(8,128)} %pop_ref.1), custom_call_target="tpu_custom_call" | custom-call | tf_op jit(solution)/shard_map/pack/pallas_call | solution.py:567
  1.4 0.6 %collective-permute-start.2 = (f32[760,128]{1,0:T(8,128)S(1)}, f32[760,128]{1,0:T(8,128)S(1)}, u32[]{:S(2)}, u32[]{:S(2)}) collective-permute-start(f32[760,128]{1,0:T(8,128)S(1)} %get-tuple-element.22), channel_id=1, source_target_pairs={{1,2},{2,1},{5,6},{6,5},{9,10},{10,9},{13,14},{14,13},{17,18},{18,... | collective-permute-start | bytes 1167368 | tf_op jit(solution)/shard_map/ppermute | solution.py:596
  2.0 4.1 %collective-permute-start = (f32[380,128]{1,0:T(8,128)S(1)}, f32[380,128]{1,0:T(8,128)S(1)}, u32[]{:S(2)}, u32[]{:S(2)}) collective-permute-start(f32[380,128]{1,0:T(8,128)S(1)} %get-tuple-element.20), channel_id=1, source_target_pairs={{0,1},{1,0},{2,3},{3,2},{4,5},{5,4},{6,7},{7,6},{8,9},{9,8},{10,11... | collective-permute-start | bytes 583688 | tf_op jit(solution)/shard_map/ppermute | solution.py:596
  6.1 0.0 collective-permute-start.1
  6.1 0.2 rim.1
  6.3 4.0 %collective-permute-start.3 = (f32[114,128]{1,0:T(8,128)S(1)}, f32[114,128]{1,0:T(8,128)S(1)}, u32[]{:S(2)}, u32[]{:S(2)}) collective-permute-start(f32[114,128]{1,0:T(8,128)S(1)} %rim.1), channel_id=1, source_target_pairs={{3,4},{4,3},{7,8},{8,7},{11,12},{12,11},{15,16},{16,15},{19,20},{2... | collective-permute-start | bytes 175112 | tf_op jit(solution)/shard_map/ppermute | solution.py:596
  10.3 4.3 %inner.1 = (f32[19,64,256]{2,1,0:T(8,128)}, f32[19,2,8,128]{3,2,1,0:T(8,128)S(1)}, f32[19,2,8,128]{3,2,1,0:T(8,128)S(1)}, f32[80,128]{1,0:T(8,128)S(1)}, f32[19,16,256]{2,1,0:T(8,128)S(1)}) custom-call(s32[4]{0:T(128)S(4)} %get-tuple-element.15.info_ref, f32[19,2,64,128]{3,2,1,0:T(8,128)S(1)} %get-tuple-element.16.first_ref.cells_ref), custom_call_target="tpu_custom_call" | custom-call | flops 1000000000 | bytes 8000000 | tf_op jit(solution)/shard_map/inner/pallas_call | solution.py:617
  14.6 3.8 %collective-permute-done.3.far_ref = f32[114,128]{1,0:T(8,128)S(1)} collective-permute-done((f32[114,128]{1,0:T(8,128)S(1)}, f32[114,128]{1,0:T(8,128)S(1)}, u32[]{:S(2)}, u32[]{:S(2)}) %collective-permute-start.3) | collective-permute-done | bytes 58400 | tf_op jit(solution)/shard_map/ppermute | solution.py:596
  18.5 1.3 %outer.1._ = f32[19,64,256]{2,1,0:T(8,128)} custom-call(s32[4]{0:T(128)S(4)} %get-tuple-element.15.info_ref, f32[19,2,8,128]{3,2,1,0:T(8,128)S(1)} %get-tuple-element.23.next_ref, f32[80,128]{1,0:T(8,128)S(1)} %get-tuple-element.18.cross_ref, f32[19,16,256]{2,1,0:T(8,128)S(1)} %get-tuple-element.19.edge_ref, ...), custom_call_target="tpu_custom_call", output_to_operand_aliasing={{}: (5, {})} | custom-call | flops 100000000 | bytes 1000000 | tf_op jit(solution)/shard_map/outer/pallas_call | solution.py:641
  19.8 0.0 collective-permute-done.one_ref
  19.8 0.0 collective-permute-done.1.more_ref
  19.8 0.0 collective-permute-done.2.two_ref
  19.8 2.4 %tail.1 = f32[19,64,256]{2,1,0:T(8,128)} custom-call(s32[4]{0:T(128)S(4)} %get-tuple-element.15.info_ref, f32[19,2,8,128]{3,2,1,0:T(8,128)S(1)} %get-tuple-element.17.own_ref, f32[80,128]{1,0:T(8,128)S(1)} %get-tuple-element.18.cross_ref, f32[19,16,256]{2,1,0:T(8,128)S(1)} %get-tuple-element.19.edge_ref, ...), custom_call_target="tpu_custom_call", output_to_operand_aliasing={{}: (7, {})} | custom-call | flops 100000000 | bytes 1000000 | tf_op jit(solution)/shard_map/tail/pallas_call | solution.py:656
Async XLA Ops:
  1.4 18.4 %collective-permute-start.2 = (f32[760,128]{1,0:T(8,128)S(1)}, f32[760,128]{1,0:T(8,128)S(1)}, u32[]{:S(2)}, u32[]{:S(2)}) collective-permute-start(f32[760,128]{1,0:T(8,128)S(1)} %get-tuple-element.22), channel_id=1, source_target_pairs={{1,2},{2,1},{5,6},{6,5},{9,10},{10,9},{13,14},{14,13},{17,18},{18,... | collective-permute-start | bytes 1167368 | tf_op jit(solution)/shard_map/ppermute | solution.py:596
  2.0 17.8 %collective-permute-start = (f32[380,128]{1,0:T(8,128)S(1)}, f32[380,128]{1,0:T(8,128)S(1)}, u32[]{:S(2)}, u32[]{:S(2)}) collective-permute-start(f32[380,128]{1,0:T(8,128)S(1)} %get-tuple-element.20), channel_id=1, source_target_pairs={{0,1},{1,0},{2,3},{3,2},{4,5},{5,4},{6,7},{7,6},{8,9},{9,8},{10,11... | collective-permute-start | bytes 583688 | tf_op jit(solution)/shard_map/ppermute | solution.py:596
  6.1 13.7 %collective-permute-start.1 = (f32[380,128]{1,0:T(8,128)S(1)}, f32[380,128]{1,0:T(8,128)S(1)}, u32[]{:S(2)}, u32[]{:S(2)}) collective-permute-start(f32[380,128]{1,0:T(8,128)S(1)} %get-tuple-element.21), channel_id=1, source_target_pairs={{0,1},{1,0},{2,3},{3,2},{4,5},{5,4},{6,7},{7,6},{8,9},{9,8},{10,11... | collective-permute-start | bytes 583688 | tf_op jit(solution)/shard_map/ppermute | solution.py:596
  6.3 12.1 %collective-permute-start.3 = (f32[114,128]{1,0:T(8,128)S(1)}, f32[114,128]{1,0:T(8,128)S(1)}, u32[]{:S(2)}, u32[]{:S(2)}) collective-permute-start(f32[114,128]{1,0:T(8,128)S(1)} %rim.1), channel_id=1, source_target_pairs={{3,4},{4,3},{7,8},{8,7},{11,12},{12,11},{15,16},{16,15},{19,20},{2... | collective-permute-start | bytes 175112 | tf_op jit(solution)/shard_map/ppermute | solution.py:596

commit v2 on v1

--- a/solution.py
+++ b/solution.py
@@ -18,7 +18,7 @@
 PAD = 8
 STRIP = 72
 MID = 32
-SPLIT = 10
+SPLIT = 12
 TOWARD = {0: (6, 7, 8, 9, 10), 1: (1, 2, 3, 4, 5)}
 LEVEL = (0, 11, 12, 13, 14, 15, 16, 17, 18)
 
@@ -389,58 +389,18 @@
     return copy
 
 
-def outer_kernel(
-    sub_count, info_ref, next_ref, cross_ref, edge_ref, far_ref, _, out_ref, strip_ref, done_ref, sem,
-):
-    sub = lax.axis_index("sub")
-    held_old, offset = info_ref[0], info_ref[2]
-
-    def end(side):
-        beside, own, border = (PAD, PAD + STEPS, PAD + 8) if side == 0 else (PAD + STEPS, PAD, PAD - 1)
-        for direction, half, at, first, count in rim_parts(1 - side):
-            strip_ref[0, direction, half, beside + first : beside + first + count, :] = far_ref[at : at + count, :]
-        for direction in range(DIRS):
-            for half in range(HALVES):
-                strip_ref[0, direction, half, own : own + STEPS, :] = next_ref[
-                    direction, half, side * STEPS : (side + 1) * STEPS, :
-                ]
-        for step in range(STEPS):
-            for at in range(5):
-                for half in range(HALVES):
-                    strip_ref[step, TOWARD[side][at], half, border, :] = cross_ref[
-                        ((step * 2 + side) * 5 + at) * HALVES + half, :
-                    ]
-        tables = moves()
-
-        def body(step, carry):
-            relaxed = shift([collide(half) for half in fetch(strip_ref.at[step], PAD, 1)], tables)
-            store(strip_ref.at[step + 1], PAD, relaxed)
-            return carry
-
-        lax.fori_loop(0, STEPS - 1, body, 0)
-        start, row = (PAD + STEPS, 0) if side == 0 else (PAD - STEPS, held_old - 8 - offset)
-        finish(side, strip_ref.at[STEPS - 1], (0, start), [], row, edge_ref, out_ref, done_ref, sem).wait()
-
-    @pl.when(sub == 0)
-    def _():
-        end(0)
-
-    @pl.when(sub == sub_count - 1)
-    def _():
-        end(1)
-
-
 def tail_kernel(
-    sub_count, info_ref, own_ref, cross_ref, edge_ref, one_ref, more_ref, two_ref, _, out_ref,
-    strip_ref, left_ref, right_ref, sem,
+    sub_count, info_ref, own_ref, next_ref, cross_ref, edge_ref, one_ref, also_ref, more_ref, two_ref, far_ref, _, out_ref,
+    strip_ref, first_raw_ref, second_raw_ref, left_ref, right_ref, sem,
 ):
     sub = lax.axis_index("sub")
     held_old, held_new, offset = info_ref[0], info_ref[1], info_ref[2]
     gained = offset + held_new - held_old
     lefts = jnp.where(offset == 0, 1, jnp.where(offset < 0, 3, 0))
     rights = jnp.where(gained == 0, 1, jnp.where(gained > 0, 3, 0))
-    lefts = jnp.where(sub == 0, 0, lefts)
-    rights = jnp.where(sub == sub_count - 1, 0, rights)
+    outer_left, outer_right = sub == 0, sub == sub_count - 1
+    inner_left, inner_right = jnp.logical_not(outer_left), jnp.logical_not(outer_right)
+    outer = jnp.logical_or(outer_left, outer_right)
     even = sub % 2 == 0
     odd = jnp.logical_not(even)
 
@@ -452,29 +412,59 @@
 
     low, high, rest = MID - STEPS - REACH, MID + 8 + STEPS, REACH - SPLIT
 
-    for here, count, start, light in ((odd, lefts, low, False), (even, rights, high, True)):
+    later = sub // 2 % 2 == 1
+    sooner = jnp.logical_not(later)
+
+    for source, when in ((one_ref, sooner), (also_ref, later)):
+        for here, count, start, right in ((odd, lefts, low, False), (even, rights, high, True)):
+
+            @pl.when(both(both(here, when), count == 3))
+            def _():
+                place(source, SPLIT, 0, SPLIT, start)
+
+            if right:
+
+                @pl.when(both(both(here, when), count == 1))
+                def _():
+                    place(source, SPLIT, 0, STEPS, start)
+
+    for here, count, start, right in ((odd, lefts, low, False), (even, rights, high, True)):
 
         @pl.when(both(here, count == 3))
         def _():
-            place(one_ref, SPLIT, 0, SPLIT, start)
             place(more_ref, rest, 0, rest, start + SPLIT)
 
+        if not right:
+
+            @pl.when(both(here, count == 1))
+            def _():
+                place(more_ref, rest, rest - STEPS, STEPS, start + REACH - STEPS)
+
+    for here, count, start, first in (
+        (both(even, inner_left), lefts, low, REACH - STEPS),
+        (both(odd, inner_right), rights, high, 0),
+    ):
+
+        @pl.when(both(here, count == 3))
+        def _():
+            place(two_ref, REACH, 0, REACH, start)
+
         @pl.when(both(here, count == 1))
         def _():
-            if light:
-                place(one_ref, SPLIT, 0, STEPS, start)
-            else:
-                place(more_ref, rest, rest - STEPS, STEPS, start + REACH - STEPS)
-
-    for here, count, start, first in ((even, lefts, low, REACH - STEPS), (odd, rights, high, 0)):
-
-        @pl.when(both(here, count == 3))
-        def _():
-            place(two_ref, REACH, 0, REACH, start)
-
-        @pl.when(both(here, count == 1))
-        def _():
             place(two_ref, REACH, first, STEPS, start + first)
+
+    for side, here in ((0, outer_left), (1, outer_right)):
+
+        @pl.when(here)
+        def _():
+            beside, own = (MID - 8, MID - STEPS) if side == 0 else (MID + 8 + STEPS, MID + 8)
+            for direction, half, at, first, count in rim_parts(1 - side):
+                strip_ref[1, direction, half, beside + first : beside + first + count, :] = far_ref[at : at + count, :]
+            for direction in range(DIRS):
+                for half in range(HALVES):
+                    strip_ref[1, direction, half, own : own + STEPS, :] = next_ref[
+                        direction, half, side * STEPS : (side + 1) * STEPS, :
+                    ]
 
     for side, count, start, border in ((0, lefts, MID - STEPS, MID), (1, rights, MID + 8, MID + 7)):
 
@@ -493,26 +483,67 @@
                         ]
 
     tables = moves()
-    work = lefts + rights
-
-    def row_of(at):
-        return pl.multiple_of(jnp.where(at < lefts, MID - 8 * (lefts - at), MID + 8 + 8 * (at - lefts)), 8)
-
-    for groups in (1, 2, 3, 4, 6):
-
-        @pl.when(work == groups)
-        def _():
-            rows = [row_of(at) for at in range(groups)]
-
-            def body(step, carry):
-                moved = jnp.minimum(step, 1)
-                cells = [fetch(strip_ref.at[step], row, moved) for row in rows]
-                relaxed = [shift([collide(half) for half in halves], tables) for halves in cells]
-                for row, halves in zip(rows, relaxed):
-                    store(strip_ref.at[step + 1], row, halves)
-                return carry
-
-            lax.fori_loop(0, STEPS, body, 0)
+    swap = jnp.where(outer, outer_left, lefts < rights)
+    firsts, seconds = jnp.where(swap, rights, lefts), jnp.where(swap, lefts, rights)
+    skip = jnp.where(outer, 1, 0)
+    left_row, right_row = MID - 8 * lefts, MID + 8
+    first_row = pl.multiple_of(jnp.where(swap, right_row, left_row), 8)
+    second_row = pl.multiple_of(jnp.where(swap, left_row, right_row), 8)
+
+    def plain(row, count, start):
+        rows = [row + 8 * at for at in range(count)]
+
+        def body(step, carry):
+            cells = [fetch(strip_ref.at[step], at, jnp.minimum(step, 1)) for at in rows]
+            relaxed = [shift([collide(half) for half in halves], tables) for halves in cells]
+            for at, halves in zip(rows, relaxed):
+                store(strip_ref.at[step + 1], at, halves)
+            return carry
+
+        lax.fori_loop(start, STEPS, body, 0)
+
+    def staggered(first_count, second_count):
+        one = (first_raw_ref, [first_row + 8 * at for at in range(first_count)])
+        two = (second_raw_ref, [second_row + 8 * at for at in range(second_count)])
+
+        def half_step(step, collided, settled, into):
+            raw_out, rows = collided
+            raw_in, to = settled
+            waiting = [fetch(raw_in, 8 * at, 0) for at in range(len(to))]
+            cells = [fetch(strip_ref.at[step], at, jnp.minimum(step, 1)) for at in rows]
+            moved = [shift(halves, tables) for halves in waiting]
+            relaxed = [[collide(half) for half in halves] for halves in cells]
+            for at, halves in zip(to, moved):
+                store(strip_ref.at[into], at, halves)
+            for at, halves in enumerate(relaxed):
+                store(raw_out, 8 * at, halves)
+
+        def body(step, carry):
+            half_step(step, one, two, jnp.where(step <= skip, STEPS + 1, step))
+            half_step(step, two, one, step + 1)
+            return carry
+
+        lax.fori_loop(0, STEPS, body, 0)
+        raw, rows = two
+        moved = [shift(fetch(raw, 8 * at, 0), tables) for at in range(len(rows))]
+        for at, halves in zip(rows, moved):
+            store(strip_ref.at[STEPS], at, halves)
+
+    for first_count, second_count in ((1, 1), (3, 1), (3, 3)):
+
+        @pl.when(both(firsts == first_count, seconds == second_count))
+        def _():
+            staggered(first_count, second_count)
+
+    for count in (1, 3):
+
+        @pl.when(both(firsts == count, seconds == 0))
+        def _():
+            plain(first_row, count, 0)
+
+    @pl.when(both(firsts == 0, seconds == 1))
+    def _():
+        plain(second_row, 1, skip)
 
     final = strip_ref.at[STEPS]
     first, last = MID - STEPS, MID + STEPS
@@ -601,8 +632,12 @@
         after = (at + 1) % total
         into = across if after % sub_count == 0 else between
         into += [(at, after), (after, at)]
-    one = send(one, inside)
+    sooner = [(at, beside) for at, beside in inside if at % sub_count // 2 % 2 == 0]
+    later = [(at, beside) for at, beside in inside if at % sub_count // 2 % 2 == 1]
+    ends = one
+    one = send(ends, everyone(sooner))
     two = send(two, everyone(between))
+    also = send(ends, everyone(later))
     rim = pl.pallas_call(
         functools.partial(rim_kernel, sub_count),
         out_shape=local(RIM, LANES),
@@ -638,37 +673,24 @@
         name="inner",
     )(info, cells)
     own, following, cross, edge = map(near, (own, following, cross, edge))
-    result = pl.pallas_call(
-        functools.partial(outer_kernel, sub_count),
-        out_shape=whole,
-        in_specs=[smem, vmem, vmem, vmem, vmem, hbm],
-        out_specs=hbm,
-        scratch_shapes=[
-            pltpu.VMEM((STEPS, DIRS, HALVES, 3 * PAD, LANES), jnp.float32),
-            pltpu.VMEM((DIRS, 8, HALVES * LANES), jnp.float32),
-            pltpu.SemaphoreType.DMA,
-        ],
-        input_output_aliases={5: 0},
-        compiler_params=params,
-        cost_estimate=pl.CostEstimate(flops=10**8, bytes_accessed=10**6, transcendentals=0),
-        name="outer",
-    )(info, following, cross, edge, near(rim), result)
     return pl.pallas_call(
         functools.partial(tail_kernel, sub_count),
         out_shape=whole,
-        in_specs=[smem] + [vmem] * 6 + [hbm],
+        in_specs=[smem] + [vmem] * 9 + [hbm],
         out_specs=hbm,
         scratch_shapes=[
-            pltpu.VMEM((STEPS + 1, DIRS, HALVES, STRIP, LANES), jnp.float32),
+            pltpu.VMEM((STEPS + 2, DIRS, HALVES, STRIP, LANES), jnp.float32),
+            pltpu.VMEM((DIRS, HALVES, 24, LANES), jnp.float32),
+            pltpu.VMEM((DIRS, HALVES, 24, LANES), jnp.float32),
             pltpu.VMEM((DIRS, 24, HALVES * LANES), jnp.float32),
             pltpu.VMEM((DIRS, 24, HALVES * LANES), jnp.float32),
             pltpu.SemaphoreType.DMA((2,)),
         ],
-        input_output_aliases={7: 0},
+        input_output_aliases={10: 0},
         compiler_params=params,
         cost_estimate=pl.CostEstimate(flops=10**8, bytes_accessed=10**6, transcendentals=0),
         name="tail",
-    )(info, own, cross, edge, near(one), near(more), near(two), result)
+    )(info, own, following, cross, edge, *map(near, (one, also, more, two, rim)), result)
 
 
 def solution(mesh):

time: 22.4 us -> 22.6 us (level)
  waiting for transfers between devices: 3.83 us -> 4.9 us
  Pallas kernels: 9.64 us -> 8.69 us
    pallas_call x1 -> x0, Pallas kernels: 1.31 us -> none  [shards(): pl.pallas_call(functools.partial(outer_kernel, sub_count), out_shape=whol...]
    ppermute x4 -> x5, waiting for transfers between devices: 3.83 us -> 4.9 us  [send(): return lax.ppermute(value, axes, pairs)]
    pallas_call x1, Pallas kernels: 2.39 us -> 2.76 us  [shards(): pl.pallas_call(functools.partial(tail_kernel, sub_count), out_shape=whole...]
    ppermute x4 -> x5, starting transfers between devices: 8.67 us -> 8.76 us  [send(): return lax.ppermute(value, axes, pairs)]
  transfers between devices with their start and end apart: 4 -> 5, of which waited for: 1 -> 1; matrix products, arithmetic and copies ran while one was open for 0% -> 0% of each run, Pallas kernels for 26% -> 20%
where the time goes in v2:
time: 22.6 us; the launch traced here: 22.4 us
  starting transfers between devices  8.76 us (39%)
  Pallas kernels  8.69 us (38%)
  waiting for transfers between devices  4.9 us (22%)
    ppermute x5, starting transfers between devices, send(): return lax.ppermute(value, axes, pairs)  8.76 us
    ppermute x5, waiting for transfers between devices, send(): return lax.ppermute(value, axes, pairs)  4.9 us
    pallas_call x1, Pallas kernels, shards(): pl.pallas_call(functools.partial(inner_kernel, slots), out_shape=(whole,...  4.34 us
    pallas_call x1, Pallas kernels, shards(): pl.pallas_call(functools.partial(tail_kernel, sub_count), out_shape=whole...  2.76 us
    pallas_call x1, Pallas kernels, shards(): pl.pallas_call(functools.partial(pack_kernel, sub_count), out_shape=(loca...  1.4 us
  transfers between devices with their start and end apart: 5, of which 1 were waited for; matrix products, arithmetic and copies ran while one was open for 0% of the time, Pallas kernels for 20%

profile of v2, /device:TPU:0, one launch (start us, length us, event | category | flops | bytes accessed | tf_op | source)
XLA Modules:
  0.0 22.4 jit_solution(8318532348210016709)
XLA Ops:
  0.0 1.4 %pack.1 = (f32[456,128]{1,0:T(8,128)S(1)}, f32[304,128]{1,0:T(8,128)S(1)}, f32[760,128]{1,0:T(8,128)S(1)}, f32[19,2,64,128]{3,2,1,0:T(8,128)S(1)}, s32[4]{0:T(128)S(4)}) custom-call(s32[4,8]{1,0:T(4,128)} %bitcast.2, s32[4,8]{1,0:T(4,128)} %bitcast.3, f32[19,64,256]{2,1,0:T(8,128)} %pop_ref.1), custom_call_target="tpu_custom_call" | custom-call | tf_op jit(solution)/shard_map/pack/pallas_call | solution.py:598
  1.4 0.6 %collective-permute-start.3 = (f32[760,128]{1,0:T(8,128)S(1)}, f32[760,128]{1,0:T(8,128)S(1)}, u32[]{:S(2)}, u32[]{:S(2)}) collective-permute-start(f32[760,128]{1,0:T(8,128)S(1)} %get-tuple-element.23), channel_id=1, source_target_pairs={{1,2},{2,1},{5,6},{6,5},{9,10},{10,9},{13,14},{14,13},{17,18},{18,... | collective-permute-start | bytes 1167368 | tf_op jit(solution)/shard_map/ppermute | solution.py:627
  2.0 4.1 %collective-permute-start = (f32[456,128]{1,0:T(8,128)S(1)}, f32[456,128]{1,0:T(8,128)S(1)}, u32[]{:S(2)}, u32[]{:S(2)}) collective-permute-start(f32[456,128]{1,0:T(8,128)S(1)} %get-tuple-element.21), channel_id=1, source_target_pairs={{0,1},{1,0},{4,5},{5,4},{8,9},{9,8},{12,13},{13,12},{16,17},{17,16... | collective-permute-start | bytes 700424 | tf_op jit(solution)/shard_map/ppermute | solution.py:627
  6.1 0.0 collective-permute-start.1
  6.1 0.0 collective-permute-start.2
  6.1 0.2 rim.1
  6.3 4.0 %collective-permute-start.4 = (f32[114,128]{1,0:T(8,128)S(1)}, f32[114,128]{1,0:T(8,128)S(1)}, u32[]{:S(2)}, u32[]{:S(2)}) collective-permute-start(f32[114,128]{1,0:T(8,128)S(1)} %rim.1), channel_id=1, source_target_pairs={{3,4},{4,3},{7,8},{8,7},{11,12},{12,11},{15,16},{16,15},{19,20},{2... | collective-permute-start | bytes 175112 | tf_op jit(solution)/shard_map/ppermute | solution.py:627
  10.4 4.3 %inner.1 = (f32[19,64,256]{2,1,0:T(8,128)}, f32[19,2,8,128]{3,2,1,0:T(8,128)S(1)}, f32[19,2,8,128]{3,2,1,0:T(8,128)S(1)}, f32[80,128]{1,0:T(8,128)S(1)}, f32[19,16,256]{2,1,0:T(8,128)S(1)}) custom-call(s32[4]{0:T(128)S(4)} %get-tuple-element.15.info_ref, f32[19,2,64,128]{3,2,1,0:T(8,128)S(1)} %get-tuple-element.16.first_ref.cells_ref), custom_call_target="tpu_custom_call" | custom-call | flops 1000000000 | bytes 8000000 | tf_op jit(solution)/shard_map/inner/pallas_call | solution.py:652
  14.7 4.9 %collective-permute-done.4.far_ref = f32[114,128]{1,0:T(8,128)S(1)} collective-permute-done((f32[114,128]{1,0:T(8,128)S(1)}, f32[114,128]{1,0:T(8,128)S(1)}, u32[]{:S(2)}, u32[]{:S(2)}) %collective-permute-start.4) | collective-permute-done | bytes 58400 | tf_op jit(solution)/shard_map/ppermute | solution.py:627
  19.6 0.0 collective-permute-done.2.more_ref
  19.6 0.0 collective-permute-done.one_ref
  19.6 0.0 collective-permute-done.1.also_ref
  19.6 0.0 collective-permute-done.3.two_ref
  19.6 2.8 %tail.1 = f32[19,64,256]{2,1,0:T(8,128)} custom-call(s32[4]{0:T(128)S(4)} %get-tuple-element.15.info_ref, f32[19,2,8,128]{3,2,1,0:T(8,128)S(1)} %get-tuple-element.17.own_ref, f32[19,2,8,128]{3,2,1,0:T(8,128)S(1)} %get-tuple-element.18.next_ref, f32[80,128]{1,0:T(8,128)S(1)} %get-tuple-element.19.cross_ref, ...), custom_call_target="tpu_custom_call", output_to_operand_aliasing={{}: (10, {})} | custom-call | flops 100000000 | bytes 1000000 | tf_op jit(solution)/shard_map/tail/pallas_call | solution.py:676
Async XLA Ops:
  1.4 18.2 %collective-permute-start.3 = (f32[760,128]{1,0:T(8,128)S(1)}, f32[760,128]{1,0:T(8,128)S(1)}, u32[]{:S(2)}, u32[]{:S(2)}) collective-permute-start(f32[760,128]{1,0:T(8,128)S(1)} %get-tuple-element.23), channel_id=1, source_target_pairs={{1,2},{2,1},{5,6},{6,5},{9,10},{10,9},{13,14},{14,13},{17,18},{18,... | collective-permute-start | bytes 1167368 | tf_op jit(solution)/shard_map/ppermute | solution.py:627
  2.0 17.7 %collective-permute-start = (f32[456,128]{1,0:T(8,128)S(1)}, f32[456,128]{1,0:T(8,128)S(1)}, u32[]{:S(2)}, u32[]{:S(2)}) collective-permute-start(f32[456,128]{1,0:T(8,128)S(1)} %get-tuple-element.21), channel_id=1, source_target_pairs={{0,1},{1,0},{4,5},{5,4},{8,9},{9,8},{12,13},{13,12},{16,17},{17,16... | collective-permute-start | bytes 700424 | tf_op jit(solution)/shard_map/ppermute | solution.py:627
  6.1 13.5 %collective-permute-start.1 = (f32[456,128]{1,0:T(8,128)S(1)}, f32[456,128]{1,0:T(8,128)S(1)}, u32[]{:S(2)}, u32[]{:S(2)}) collective-permute-start(f32[456,128]{1,0:T(8,128)S(1)} %get-tuple-element.21), channel_id=1, source_target_pairs={{2,3},{3,2},{6,7},{7,6},{10,11},{11,10},{14,15},{15,14},{18,19},{1... | collective-permute-start | bytes 700424 | tf_op jit(solution)/shard_map/ppermute | solution.py:627
  6.1 13.5 %collective-permute-start.2 = (f32[304,128]{1,0:T(8,128)S(1)}, f32[304,128]{1,0:T(8,128)S(1)}, u32[]{:S(2)}, u32[]{:S(2)}) collective-permute-start(f32[304,128]{1,0:T(8,128)S(1)} %get-tuple-element.22), channel_id=1, source_target_pairs={{0,1},{1,0},{2,3},{3,2},{4,5},{5,4},{6,7},{7,6},{8,9},{9,8},{10,11... | collective-permute-start | bytes 466952 | tf_op jit(solution)/shard_map/ppermute | solution.py:627
  6.3 13.3 %collective-permute-start.4 = (f32[114,128]{1,0:T(8,128)S(1)}, f32[114,128]{1,0:T(8,128)S(1)}, u32[]{:S(2)}, u32[]{:S(2)}) collective-permute-start(f32[114,128]{1,0:T(8,128)S(1)} %rim.1), channel_id=1, source_target_pairs={{3,4},{4,3},{7,8},{8,7},{11,12},{12,11},{15,16},{16,15},{19,20},{2... | collective-permute-start | bytes 175112 | tf_op jit(solution)/shard_map/ppermute | solution.py:627
